TPU v7x, 32 devices: a whole 2x2x4 slice. The times are simulated.
32 devices in a mesh: beam: 2 (over y), chan: 8 (over z, x), tm: 2 (over core).
Axes of the slice: x: 2, y: 2, z: 4, core: 2. Of those that a mesh axis runs over, the one named last changes fastest.
Arguments:
- spectra: float32 [512, 8192], P(('beam', 'chan'), 'tm'), parts along dimension 0, may hold values from -6 to 6
- delay_shifts: int32 [8, 256], replicated, may hold values from 0 to 112, as said below
- box_widths: int32 [20], replicated, may hold values from 1 to 128, as said below
Outputs:
- pulse_power: float32 [512, 8192], P(('beam', 'chan'), 'tm'), parts along dimension 0
There are 2 independent parts, one for each index of `beam`. A program takes and returns all parts, laid end to end along the dimension named above; an argument that names none is the same for every part. Nothing has to cross between parts.
Inputs may be any that keep to these rules, and one draw needn't show every extreme that they name: `delay_shifts`: each section's row of the table contains 112 in some column. `box_widths`: some filter has width 128.
All inputs are finite; a program needn't handle non-finite values.
Results may differ from a plain program's by a relative error of at most 0.000023.
Values sent between devices are 32-bit elements; how exact they have to be, the bound alone decides.
No kernel may reach another device: no remote copies, remote signals or barrier semaphores. Data moves between devices by JAX's collectives and lax.ppermute only.
A program may use at most 64 MiB of HBM per device.

v0:
```python
import jax
import jax.numpy as jnp
from jax import lax
from jax.sharding import PartitionSpec as P

LOCAL_SECTIONS = 5
SWAP_SECTIONS = 3
TAIL = 1024
SHIFT_MAX = 112
WMAX = 128
NBOX = 20


root_half = 0.7071067811865476


def from_behind(x, axis, by):
    peers = lax.axis_size(axis)
    pairs = [(i, i + by) for i in range(peers) if 0 <= i + by < peers]
    return lax.ppermute(x, axis, pairs)


def swapped(block, axis, bit):
    count = lax.axis_size(axis)
    route = []
    for low in range(count):
        high = low | 1 << bit
        if high != low and high < count:
            route += [(low, high), (high, low)]
    return lax.ppermute(block, axis, route)


def pair_rows(series, stride):
    total_rows, length = series.shape
    paired = series.reshape(total_rows // (2 * stride), 2, stride, length)
    lower = jnp.broadcast_to(paired[:, 0:1], paired.shape).reshape(total_rows, length)
    upper = jnp.broadcast_to(paired[:, 1:2], paired.shape).reshape(total_rows, length)
    return (lower, upper)


def delay_add(lower, upper_wide, shifts):
    current = upper_wide
    bit_count = SHIFT_MAX.bit_length()
    for bit_place in range(bit_count):
        amount = 2**bit_place
        moved = jnp.concatenate(
            [jnp.zeros((current.shape[0], amount), current.dtype), current[:, :-amount]], axis=1
        )
        take_moved = (shifts >> bit_place & 1)[:, None] == 1
        current = jnp.where(take_moved, moved, current)
    delayed = current[:, SHIFT_MAX:]
    return (lower + delayed) * root_half


def widen_upper(upper):
    earlier = jnp.zeros((upper.shape[0], SHIFT_MAX), upper.dtype)
    return jnp.concatenate([earlier, upper], axis=1)


def boxcar_power(segment, box_widths):
    length = segment.shape[1] - WMAX
    running = jnp.cumsum(segment, axis=1)
    closing = running[:, WMAX:]

    def add_filter(which, summed):
        span_width = box_widths[which]
        opening = lax.dynamic_slice_in_dim(running, WMAX - span_width, length, 1)
        window_sum = closing - opening
        return summed + window_sum * window_sum / span_width.astype(jnp.float32)

    summed = lax.fori_loop(0, NBOX, add_filter, jnp.zeros(closing.shape, jnp.float32))
    return summed / NBOX


def local(spectra, delay_shifts, box_widths):
    ch_rows, time_len = spectra.shape
    row_start = lax.axis_index("chan") * ch_rows
    own_shifts = lax.dynamic_slice_in_dim(delay_shifts, row_start, ch_rows, 1)
    earlier = from_behind(spectra[:, -TAIL:], "tm", 1)
    series = jnp.concatenate([earlier, spectra], axis=1)
    for level in range(LOCAL_SECTIONS):
        lower, upper = pair_rows(series, 2**level)
        series = delay_add(lower, widen_upper(upper), own_shifts[level])
    chan_bits = lax.axis_size("chan").bit_length() - 1
    for swap_step in range(SWAP_SECTIONS):
        bit_place = chan_bits - SWAP_SECTIONS + swap_step
        partner = swapped(series, "chan", bit_place)
        own_bit = lax.axis_index("chan") >> bit_place & 1
        lower = jnp.where(own_bit == 0, series, partner)
        upper = jnp.where(own_bit == 0, partner, series)
        series = delay_add(lower, widen_upper(upper), own_shifts[LOCAL_SECTIONS + swap_step])
    segment = series[:, TAIL - WMAX :]
    return boxcar_power(segment, box_widths)


def solution(mesh):
    in_specs = (P(("beam", "chan"), "tm"), P(), P())
    out_specs = P(("beam", "chan"), "tm")
    return jax.shard_map(local, mesh=mesh, in_specs=in_specs, out_specs=out_specs, check_vma=False)
```

profile of v0, /device:TPU:0, one launch (start us, length us, event | category | flops | bytes accessed | tf_op | source)
XLA Modules:
  0.0 169.1 jit_solution(4183025125275528850)
XLA Ops:
  0.0 0.9 slice.261
  0.9 2.4 %collective-permute-start = (f32[32,1024]{1,0:T(8,128)S(1)}, f32[32,1024]{1,0:T(8,128)S(1)}, u32[]{:S(2)}, u32[]{:S(2)}) collective-permute-start(f32[32,1024]{1,0:T(8,128)S(1)} %slice.261), channel_id=1, source_target_pairs={{0,1},{2,3},{4,5},{6,7},{8,9},{10,11},{12,13},{14,15},{16,17},{18,... | collective-permute-start | bytes 393224 | tf_op jit(solution)/shard_map/ppermute | solution.py:20
  3.5 0.8 collective-permute-done
  4.3 1.1 pad_maximum_fusion
  22.4 2.4 %collective-permute-start.1 = (f32[32,5120]{1,0:T(8,128)S(1)}, f32[32,5120]{1,0:T(8,128)S(1)}, u32[]{:S(2)}, u32[]{:S(2)}) collective-permute-start(f32[32,5120]{1,0:T(8,128)S(1)} %fusion.5), channel_id=1, source_target_pairs={{0,2},{2,0},{4,6},{6,4},{8,10},{10,8},{12,14},{14,12},{1,3},{3,1},... | collective-permute-start | bytes 1966088 | tf_op jit(solution)/shard_map/ppermute | solution.py:30
  24.8 15.3 %collective-permute-done.1 = f32[32,5120]{1,0:T(8,128)S(1)} collective-permute-done((f32[32,5120]{1,0:T(8,128)S(1)}, f32[32,5120]{1,0:T(8,128)S(1)}, u32[]{:S(2)}, u32[]{:S(2)}) %collective-permute-start.1) | collective-permute-done | bytes 655392 | tf_op jit(solution)/shard_map/ppermute | solution.py:30
  42.4 1.9 %collective-permute-start.2 = (f32[32,5120]{1,0:T(8,128)S(1)}, f32[32,5120]{1,0:T(8,128)S(1)}, u32[]{:S(2)}, u32[]{:S(2)}) collective-permute-start(f32[32,5120]{1,0:T(8,128)S(1)} %fusion.3), channel_id=1, source_target_pairs={{0,4},{4,0},{2,6},{6,2},{8,12},{12,8},{10,14},{14,10},{1,5},{5,1},... | collective-permute-start | bytes 1966088 | tf_op jit(solution)/shard_map/ppermute | solution.py:30
  44.3 14.6 %collective-permute-done.2 = f32[32,5120]{1,0:T(8,128)S(1)} collective-permute-done((f32[32,5120]{1,0:T(8,128)S(1)}, f32[32,5120]{1,0:T(8,128)S(1)}, u32[]{:S(2)}, u32[]{:S(2)}) %collective-permute-start.2) | collective-permute-done | bytes 655392 | tf_op jit(solution)/shard_map/ppermute | solution.py:30
  61.3 2.6 %collective-permute-start.3 = (f32[32,5120]{1,0:T(8,128)S(1)}, f32[32,5120]{1,0:T(8,128)S(1)}, u32[]{:S(2)}, u32[]{:S(2)}) collective-permute-start(f32[32,5120]{1,0:T(8,128)S(1)} %fusion.1), channel_id=1, source_target_pairs={{0,8},{8,0},{2,10},{10,2},{4,12},{12,4},{6,14},{14,6},{1,9},{9,1},... | collective-permute-start | bytes 1966088 | tf_op jit(solution)/shard_map/ppermute | solution.py:30
  63.9 28.0 %collective-permute-done.3 = f32[32,5120]{1,0:T(8,128)S(1)} collective-permute-done((f32[32,5120]{1,0:T(8,128)S(1)}, f32[32,5120]{1,0:T(8,128)S(1)}, u32[]{:S(2)}, u32[]{:S(2)}) %collective-permute-start.3) | collective-permute-done | bytes 655392 | tf_op jit(solution)/shard_map/ppermute | solution.py:30
  94.4 9.3 %reduce-window.6 = f32[32,33,128]{2,1,0:T(8,128)S(1)} reduce-window(f32[32,33,128]{2,1,0:T(8,128)S(1)} %reshape.859, f32[]{:T(128)} %constant.88.clone.1), window={size=1x1x128 pad=0_0x0_0x127_0}, to_apply=%region_0.1 | reduce-window | flops 17166336 | bytes 1081348 | tf_op jit(solution)/shard_map/reduce-window
  105.4 62.9 %while.16 = (s32[]{:T(128)}, f32[32,4096]{1,0:T(8,128)S(1)}, s32[20]{0:T(128)S(1)}, f32[32,4224]{1,0:T(8,128)S(1)}, f32[32,4096]{1,0:T(8,128)S(1)}, /*index=5*/s32[]{:T(128)}, s32[1]{0:T(128)}, s32[]{:T(128)}, s32[1]{0:T(128)}) while((s32[]{:T(128)}, f32[32,4096]{1,0:T(8,128)S(1)}, s32[20]{0:T(128)S(1)}, f32[32,4224]{1,0:T(8,128)S(1)}, ...), condition=%wide.region_3.4_spmd.clone, body=%wide.region_2.3_spmd.clone.sunk | while | flops 655368 | bytes 2097329 | solution.py:71
  111.7 0.7 dynamic_slice.31
  118.0 0.7 dynamic_slice.31
  124.3 0.7 dynamic_slice.31
  127.4 0.7 dynamic_slice.31
  130.5 0.7 dynamic_slice.31
  133.7 0.7 dynamic_slice.31
  136.8 0.7 dynamic_slice.31
  140.0 0.7 dynamic_slice.31
  143.1 0.7 dynamic_slice.31
  146.3 0.7 dynamic_slice.31
  149.4 0.7 dynamic_slice.31
  168.3 0.8 broadcast_multiply_fusion
  (137 shorter events, 39.7 us)
Async XLA Ops:
  0.0 3.4 %copy-start = (s32[8,256]{1,0:T(8,128)S(1)}, s32[8,256]{1,0:T(8,128)}, u32[]{:S(2)}) copy-start(s32[8,256]{1,0:T(8,128)} %param.6) | copy-start | bytes 24580
  0.9 3.4 %collective-permute-start = (f32[32,1024]{1,0:T(8,128)S(1)}, f32[32,1024]{1,0:T(8,128)S(1)}, u32[]{:S(2)}, u32[]{:S(2)}) collective-permute-start(f32[32,1024]{1,0:T(8,128)S(1)} %slice.261), channel_id=1, source_target_pairs={{0,1},{2,3},{4,5},{6,7},{8,9},{10,11},{12,13},{14,15},{16,17},{18,... | collective-permute-start | bytes 393224 | tf_op jit(solution)/shard_map/ppermute | solution.py:20
  22.4 17.6 %collective-permute-start.1 = (f32[32,5120]{1,0:T(8,128)S(1)}, f32[32,5120]{1,0:T(8,128)S(1)}, u32[]{:S(2)}, u32[]{:S(2)}) collective-permute-start(f32[32,5120]{1,0:T(8,128)S(1)} %fusion.5), channel_id=1, source_target_pairs={{0,2},{2,0},{4,6},{6,4},{8,10},{10,8},{12,14},{14,12},{1,3},{3,1},... | collective-permute-start | bytes 1966088 | tf_op jit(solution)/shard_map/ppermute | solution.py:30
  42.4 16.5 %collective-permute-start.2 = (f32[32,5120]{1,0:T(8,128)S(1)}, f32[32,5120]{1,0:T(8,128)S(1)}, u32[]{:S(2)}, u32[]{:S(2)}) collective-permute-start(f32[32,5120]{1,0:T(8,128)S(1)} %fusion.3), channel_id=1, source_target_pairs={{0,4},{4,0},{2,6},{6,2},{8,12},{12,8},{10,14},{14,10},{1,5},{5,1},... | collective-permute-start | bytes 1966088 | tf_op jit(solution)/shard_map/ppermute | solution.py:30
  61.3 30.6 %collective-permute-start.3 = (f32[32,5120]{1,0:T(8,128)S(1)}, f32[32,5120]{1,0:T(8,128)S(1)}, u32[]{:S(2)}, u32[]{:S(2)}) collective-permute-start(f32[32,5120]{1,0:T(8,128)S(1)} %fusion.1), channel_id=1, source_target_pairs={{0,8},{8,0},{2,10},{10,2},{4,12},{12,4},{6,14},{14,6},{1,9},{9,1},... | collective-permute-start | bytes 1966088 | tf_op jit(solution)/shard_map/ppermute | solution.py:30
  104.7 0.7 copy-start.2
  168.3 0.9 copy-start.1
where the time goes:
time: 170 us; the launch traced here: 169 us
  waiting for transfers between devices  58.6 us (34%)
  loops' own time  41.6 us (24%)
  other arithmetic  36.5 us (21%)
  local copies, waits for them, and re-layouts  22.6 us (13%)
  starting transfers between devices  9.29 us (5%)
    ppermute x3, waiting for transfers between devices, swapped(): return lax.ppermute(block, axis, route)  57.8 us
    another operation x1, loops' own time, boxcar_power(): lax.fori_loop(0, NBOX, add_filter, jnp.zeros(closing.shape, jnp.float32))  41.6 us
    select_n x48, other arithmetic, delay_add(): current = jnp.where(take_moved, moved, current)  13.2 us
    dynamic_slice x20, local copies, waits for them, and re-layouts, add_filter(): span_width = box_widths[which]  13.1 us
    another operation x3, other arithmetic  9.77 us
    add x20, other arithmetic, add_filter(): return summed + window_sum * window_sum / span_width.astype(jnp.float32)  8.21 us
    ppermute x3, starting transfers between devices, swapped(): return lax.ppermute(block, axis, route)  6.89 us
  transfers between devices with their start and end apart: 4, of which 4 were waited for; matrix products, arithmetic and copies ran while one was open for 0% of the time, Pallas kernels for 0%

commit v1 on v0

v1 whole, which is shorter than its diff:
```python
import functools

import jax
import jax.numpy as jnp
from jax import lax
from jax.experimental import pallas as pl
from jax.experimental.pallas import tpu as pltpu
from jax.sharding import PartitionSpec as P

LOCAL_SECTIONS = 5
SWAP_SECTIONS = 3
SECTIONS = LOCAL_SECTIONS + SWAP_SECTIONS
SHIFT_MAX = 112
WMAX = 128
NBOX = 20
LANES = 128
SUB = 8
NBOX_PAD = -(-NBOX // SUB) * SUB


def up_to_lanes(samples):
    return -(-samples // LANES) * LANES


def cols(k):
    return slice(k * LANES, (k + 1) * LANES)


def group_rows(g):
    return slice(g * SUB, (g + 1) * SUB)


def delay_tables(column):
    delay = jnp.broadcast_to(column, (column.shape[0], LANES))
    lane = lax.broadcasted_iota(jnp.int32, delay.shape, 1)
    return (lane - delay) & (LANES - 1), lane < LANES - delay


def shifted(newer, older, tables):
    take, fresh = tables
    mixed = jnp.where(fresh, newer, older)
    return jnp.take_along_axis(mixed, take, axis=1, mode="promise_in_bounds")


def local_kernel(earlier_ref, x_ref, table_ref, *rest):
    groups = x_ref.shape[0] // SUB
    outs, buffers = rest[:groups], rest[groups:]
    head = earlier_ref.shape[1] // LANES
    chunks = head + x_ref.shape[1] // LANES
    dropped = chunks - outs[0].shape[1] // LANES
    sub = lax.broadcasted_iota(jnp.int32, (SUB, LANES), 0)

    def read(level, g, k):
        if level:
            return buffers[(level - 1) % 2][group_rows(g), cols(k)]
        if k < head:
            return earlier_ref[group_rows(g), cols(k)]
        return x_ref[group_rows(g), cols(k - head)]

    for level in range(LOCAL_SECTIONS):
        for g in range(groups):
            tables = delay_tables(table_ref[group_rows(g), level : level + 1])
            older = jnp.zeros((SUB, LANES), jnp.float32)
            for k in range(chunks):
                if 1 << level < SUB:
                    stride = 1 << level
                    own_bit = (sub >> level & 1) == 1
                    own = read(level, g, k)
                    lower = jnp.where(own_bit, pltpu.roll(own, stride, 0), own)
                    upper = jnp.where(own_bit, own, pltpu.roll(own, SUB - stride, 0))
                else:
                    stride = (1 << level) // SUB
                    lower = read(level, g & ~stride, k)
                    upper = read(level, g | stride, k)
                value = lower + shifted(upper, older, tables)
                older = upper
                if level < LOCAL_SECTIONS - 1:
                    buffers[level % 2][group_rows(g), cols(k)] = value
                elif k >= dropped:
                    outs[g][:, cols(k - dropped)] = value


def pair_of(own_ref, partner_ref, upper_own, k):
    own, partner = own_ref[:, cols(k)], partner_ref[:, cols(k)]
    return jnp.where(upper_own, partner, own), jnp.where(upper_own, own, partner)


def bit_mask(table_ref, column):
    return jnp.broadcast_to(table_ref[:, column : column + 1], (SUB, LANES)) == 1


def swap_kernel(delay_columns, bit_column, own_ref, partner_ref, table_ref, *outs):
    dropped = (own_ref.shape[1] - outs[0].shape[1]) // LANES
    upper_own = bit_mask(table_ref, bit_column)
    for column, out_ref in zip(delay_columns, outs):
        tables = delay_tables(table_ref[:, column : column + 1])
        older = None
        for k in range(own_ref.shape[1] // LANES):
            lower, upper = pair_of(own_ref, partner_ref, upper_own, k)
            if k >= dropped:
                out_ref[:, cols(k - dropped)] = lower + shifted(upper, older, tables)
            older = upper


def power_kernel(delay_column, bit_column, own_ref, partner_ref, table_ref, width_ref, weight_ref, out_ref, prefix, suffix, total):
    chunks = out_ref.shape[1] // LANES + 1
    dropped = own_ref.shape[1] // LANES - chunks
    upper_own = bit_mask(table_ref, bit_column)
    tables = delay_tables(table_ref[:, delay_column : delay_column + 1])
    older, pieces = None, []
    for k in range(own_ref.shape[1] // LANES):
        lower, upper = pair_of(own_ref, partner_ref, upper_own, k)
        if k >= dropped:
            pieces.append(lower + shifted(upper, older, tables))
        older = upper
    source = lax.broadcasted_iota(jnp.int32, (LANES, 2 * LANES), 0)
    target = lax.broadcasted_iota(jnp.int32, (LANES, 2 * LANES), 1)
    summing = jnp.where(target < LANES, jnp.where(source <= target, 1.0, 0.0), jnp.where(source > target - LANES, -1.0, 0.0))
    sums = jnp.dot(jnp.concatenate(pieces, axis=0), summing, precision=lax.Precision.HIGHEST, preferred_element_type=jnp.float32)
    prefix[...] = sums[:, :LANES]
    suffix[...] = sums[:, LANES:]
    half = (chunks - 1) // 2

    for start in range(1, chunks, half):
        def add_filter(f, summed):
            width = jnp.broadcast_to(width_ref[pl.ds(f, 1), :], (SUB, LANES))
            weight = jnp.broadcast_to(weight_ref[pl.ds(f, 1), :], (SUB, LANES))
            lane = lax.broadcasted_iota(jnp.int32, (SUB, LANES), 1)
            tables = (lane - width) & (LANES - 1), lane < LANES - width
            updated = []
            for i, value in enumerate(summed):
                k = start + i
                here = prefix[group_rows(k), :]
                window = here - shifted(here, suffix[group_rows(k - 1), :], tables)
                updated.append(value + window * window * weight)
            return tuple(updated)

        zero = jnp.zeros((SUB, LANES), jnp.float32)
        summed = lax.fori_loop(0, NBOX, add_filter, (zero,) * half)
        for i, value in enumerate(summed):
            out_ref[:, cols(start - 1 + i)] = value


VMEM_BLOCK = pl.BlockSpec(memory_space=pltpu.VMEM)


def call(kernel, args, out_lengths, scratch=(), rows=SUB):
    shapes = [jax.ShapeDtypeStruct((rows, length), jnp.float32) for length in out_lengths]
    return pl.pallas_call(
        kernel,
        out_shape=shapes,
        in_specs=[VMEM_BLOCK] * len(args),
        out_specs=[VMEM_BLOCK] * len(shapes),
        scratch_shapes=list(scratch),
        compiler_params=pltpu.CompilerParams(vmem_limit_bytes=8 << 20),
    )(*args)


def swapped(block, flip):
    count = lax.axis_size("chan")
    return lax.ppermute(block, "chan", [(i, i ^ flip) for i in range(count)])


def local(spectra, delay_shifts, box_widths):
    ch_rows, time_len = spectra.shape
    groups = ch_rows // SUB
    steps = lax.axis_size("tm")
    me = lax.axis_index("chan")
    chan_bits = lax.axis_size("chan").bit_length() - 1
    bits = [1 << (chan_bits - SWAP_SECTIONS + i) for i in range(SWAP_SECTIONS)]

    halo = [up_to_lanes((SWAP_SECTIONS - i) * SHIFT_MAX + WMAX) for i in range(SWAP_SECTIONS)] + [WMAX]
    tail = up_to_lanes(SECTIONS * SHIFT_MAX + WMAX)
    earlier = lax.ppermute(spectra[:, -tail:], "tm", [(i, i + 1) for i in range(steps - 1)])

    own_shifts = lax.dynamic_slice_in_dim(delay_shifts, me * ch_rows, ch_rows, 1)
    peer_shifts = lax.dynamic_slice_in_dim(delay_shifts, (me ^ bits[1]) * ch_rows, ch_rows, 1)
    own_bits = jnp.stack([jnp.broadcast_to((me & bit != 0).astype(jnp.int32), (ch_rows,)) for bit in bits])
    table = jnp.concatenate([own_shifts, peer_shifts[LOCAL_SECTIONS + 1 :][:1], own_bits]).T
    widths = jnp.concatenate([box_widths, jnp.full((NBOX_PAD - NBOX,), WMAX, jnp.int32)])
    weights = 1.0 / (widths.astype(jnp.float32) * (NBOX * 2.0**SECTIONS))
    widths = jnp.broadcast_to(widths[:, None], (NBOX_PAD, LANES))
    weights = jnp.broadcast_to(weights[:, None], (NBOX_PAD, LANES))

    wide = pltpu.VMEM((ch_rows, tail + time_len), jnp.float32)
    pieces = call(local_kernel, (earlier, spectra, table), [halo[0] + time_len] * groups, (wide, wide))
    tables = [table[group_rows(g)] for g in range(groups)]
    peers = [swapped(piece, bits[0]) for piece in pieces]
    results = []
    sections = [LOCAL_SECTIONS + i for i in range(SWAP_SECTIONS)]
    for g in range(groups):
        first = functools.partial(swap_kernel, (sections[0],), SECTIONS + 1)
        (one,) = call(first, (pieces[g], peers[g], tables[g]), [halo[1] + time_len])
        one_peer = swapped(one, bits[1])
        second = functools.partial(swap_kernel, (SECTIONS, sections[1]), SECTIONS + 2)
        sent, two = call(second, (one, one_peer, tables[g]), [halo[2] + time_len] * 2)
        two_peer = swapped(sent, bits[1] | bits[2])
        third = functools.partial(power_kernel, sections[2], SECTIONS + 3)
        sums = pltpu.VMEM((SUB * (time_len // LANES + 1), LANES), jnp.float32)
        acc = pltpu.VMEM((SUB, time_len), jnp.float32)
        results += call(third, (two, two_peer, tables[g], widths, weights), [time_len], (sums, sums, acc))
    return jnp.concatenate(results, axis=0)


def solution(mesh):
    in_specs = (P(("beam", "chan"), "tm"), P(), P())
    out_specs = P(("beam", "chan"), "tm")
    return jax.shard_map(local, mesh=mesh, in_specs=in_specs, out_specs=out_specs, check_vma=False)
```

time: 170 us -> 62.7 us (0.37)
  waiting for transfers between devices: 58.6 us -> 4.6 us
  loops' own time: 41.6 us -> 0 us
  other arithmetic: 36.5 us -> 0.84 us
  starting transfers between devices: 9.29 us -> 32.8 us
  Pallas kernels: 0 us -> 20.9 us
  local copies, waits for them, and re-layouts: 22.6 us -> 3.12 us
    ppermute x4 -> x13, waiting for transfers between devices: 58.6 us -> 4.6 us  [the longest x12 4.6 us: swapped(): return lax.ppermute(block, 'chan', [(i, i ^ flip) for i in range(count)])]
    another operation x1 -> x0, loops' own time: 41.6 us -> none  [boxcar_power(): lax.fori_loop(0, NBOX, add_filter, jnp.zeros(closing.shape, jnp.float32))]
    ppermute x4 -> x13, starting transfers between devices: 9.29 us -> 32.8 us  [the longest x12 30.4 us: swapped(): return lax.ppermute(block, 'chan', [(i, i ^ flip) for i in range(count)])]
    pallas_call x0 -> x13, Pallas kernels: none -> 20.9 us  [call(): pl.pallas_call(kernel, out_shape=shapes, in_specs=[VMEM_BLOCK] * len(args...]
    select_n x51 -> x0, other arithmetic: 13.4 us -> none  [the longest x48 13.2 us: delay_add(): current = jnp.where(take_moved, moved, current)]
    dynamic_slice x21 -> x1, local copies, waits for them, and re-layouts: 13.2 us -> 0.07 us  [local(): lax.dynamic_slice_in_dim(delay_shifts, (me ^ bits[1]) * ch_rows, ch_rows, 1)]
    another operation x3 -> x0, other arithmetic: 9.77 us -> none
    add x20 -> x0, other arithmetic: 8.21 us -> none  [add_filter(): return summed + window_sum * window_sum / span_width.astype(jnp.float32)]
  transfers between devices with their start and end apart: 4 -> 13, of which waited for: 4 -> 4; matrix products, arithmetic and copies ran while one was open for 0% -> 1% of each run, Pallas kernels for 0% -> 23%
where the time goes in v1:
time: 62.7 us; the launch traced here: 62.5 us
  starting transfers between devices  32.8 us (52%)
  Pallas kernels  20.9 us (33%)
  waiting for transfers between devices  4.6 us (7%)
  local copies, waits for them, and re-layouts  3.12 us (5%)
  other arithmetic  0.84 us (1%)
    ppermute x12, starting transfers between devices, swapped(): return lax.ppermute(block, 'chan', [(i, i ^ flip) for i in range(count)])  30.4 us
    pallas_call x13, Pallas kernels, call(): pl.pallas_call(kernel, out_shape=shapes, in_specs=[VMEM_BLOCK] * len(args...  20.9 us
    ppermute x12, waiting for transfers between devices, swapped(): return lax.ppermute(block, 'chan', [(i, i ^ flip) for i in range(count)])  4.6 us
    ppermute x1, starting transfers between devices, local(): lax.ppermute(spectra[:, -tail:], 'tm', [(i, i + 1) for i in range(steps -...  2.4 us
    unnamed x8, local copies, waits for them, and re-layouts  1.9 us
  transfers between devices with their start and end apart: 13, of which 4 were waited for; matrix products, arithmetic and copies ran while one was open for 1% of the time, Pallas kernels for 23%

profile of v1, /device:TPU:0, one launch (start us, length us, event | category | flops | bytes accessed | tf_op | source)
XLA Modules:
  0.0 62.5 jit_solution(12132631188050223439)
XLA Ops:
  0.0 0.9 %slice.20 = f32[32,1024]{1,0:T(8,128)S(1)} slice(f32[32,4096]{1,0:T(8,128)} %x_ref.1), slice={[0:32], [3072:4096]} | slice | bytes 262144 | tf_op jit(solution)/shard_map/slice | solution.py:174
  0.9 2.4 %collective-permute-start = (f32[32,1024]{1,0:T(8,128)S(1)}, f32[32,1024]{1,0:T(8,128)S(1)}, u32[]{:S(2)}, u32[]{:S(2)}) collective-permute-start(f32[32,1024]{1,0:T(8,128)S(1)} %slice.20), channel_id=1, source_target_pairs={{0,1},{2,3},{4,5},{6,7},{8,9},{10,11},{12,13},{14,15},{16,17},{18,... | collective-permute-start | bytes 393224 | tf_op jit(solution)/shard_map/ppermute | solution.py:174
  3.4 0.7 %copy-done.1 = s32[8,256]{1,0:T(8,128)S(1)} copy-done((s32[8,256]{1,0:T(8,128)S(1)}, s32[8,256]{1,0:T(8,128)}, u32[]{:S(2)}) %copy-start.1) | copy-done | bytes 8216
  4.4 1.0 %copy-done = f32[32,4096]{1,0:T(8,128)S(1)} copy-done((f32[32,4096]{1,0:T(8,128)S(1)}, f32[32,4096]{1,0:T(8,128)}, u32[]{:S(2)}) %copy-start) | copy-done | bytes 524312
  5.4 2.2 %shard_map.37 = (f32[8,4608]{1,0:T(8,128)S(1)}, f32[8,4608]{1,0:T(8,128)S(1)}, f32[8,4608]{1,0:T(8,128)S(1)}, f32[8,4608]{1,0:T(8,128)S(1)}) custom-call(f32[32,1024]{1,0:T(8,128)S(1)} %collective-permute-done.earlier_ref, f32[32,4096]{1,0:T(8,128)S(1)} %copy-done, s32[32,12]{1,0:T(8,128)S(1)} %bitcast.1), custom_call_target="tpu_custom_call" | custom-call | tf_op jit(solution)/shard_map/pallas_call | solution.py:149
  7.7 2.4 %collective-permute-start.1 = (f32[8,4608]{1,0:T(8,128)S(1)}, f32[8,4608]{1,0:T(8,128)S(1)}, u32[]{:S(2)}, u32[]{:S(2)}) collective-permute-start(f32[8,4608]{1,0:T(8,128)S(1)} %get-tuple-element.17.own_ref), channel_id=1, source_target_pairs={{0,2},{2,0},{4,6},{6,4},{8,10},{10,8},{12,14},{14,12},{1,3},{3,1},... | collective-permute-start | bytes 442376 | tf_op jit(solution)/shard_map/ppermute | solution.py:161
  10.1 1.9 %collective-permute-start.7 = (f32[8,4608]{1,0:T(8,128)S(1)}, f32[8,4608]{1,0:T(8,128)S(1)}, u32[]{:S(2)}, u32[]{:S(2)}) collective-permute-start(f32[8,4608]{1,0:T(8,128)S(1)} %get-tuple-element.23.own_ref), channel_id=1, source_target_pairs={{0,2},{2,0},{4,6},{6,4},{8,10},{10,8},{12,14},{14,12},{1,3},{3,1},... | collective-permute-start | bytes 442376 | tf_op jit(solution)/shard_map/ppermute | solution.py:161
  12.2 2.6 %collective-permute-done.1.partner_ref = f32[8,4608]{1,0:T(8,128)S(1)} collective-permute-done((f32[8,4608]{1,0:T(8,128)S(1)}, f32[8,4608]{1,0:T(8,128)S(1)}, u32[]{:S(2)}, u32[]{:S(2)}) %collective-permute-start.1) | collective-permute-done | bytes 147488 | tf_op jit(solution)/shard_map/ppermute | solution.py:161
  14.9 2.2 %collective-permute-start.2 = (f32[8,4480]{1,0:T(8,128)S(1)}, f32[8,4480]{1,0:T(8,128)S(1)}, u32[]{:S(2)}, u32[]{:S(2)}) collective-permute-start(f32[8,4480]{1,0:T(8,128)S(1)} %shard_map.38.own_ref), channel_id=1, source_target_pairs={{0,4},{2,6},{4,0},{6,2},{8,12},{10,14},{12,8},{14,10},{1,5},{3,7},... | collective-permute-start | bytes 430088 | tf_op jit(solution)/shard_map/ppermute | solution.py:161
  17.1 0.8 %collective-permute-done.4.partner_ref = f32[8,4608]{1,0:T(8,128)S(1)} collective-permute-done((f32[8,4608]{1,0:T(8,128)S(1)}, f32[8,4608]{1,0:T(8,128)S(1)}, u32[]{:S(2)}, u32[]{:S(2)}) %collective-permute-start.4) | collective-permute-done | bytes 147488 | tf_op jit(solution)/shard_map/ppermute | solution.py:161
  18.1 2.2 %collective-permute-start.5 = (f32[8,4480]{1,0:T(8,128)S(1)}, f32[8,4480]{1,0:T(8,128)S(1)}, u32[]{:S(2)}, u32[]{:S(2)}) collective-permute-start(f32[8,4480]{1,0:T(8,128)S(1)} %shard_map.41.own_ref), channel_id=1, source_target_pairs={{0,4},{2,6},{4,0},{6,2},{8,12},{10,14},{12,8},{14,10},{1,5},{3,7},... | collective-permute-start | bytes 430088 | tf_op jit(solution)/shard_map/ppermute | solution.py:161
  20.3 0.8 %collective-permute-done.7.partner_ref = f32[8,4608]{1,0:T(8,128)S(1)} collective-permute-done((f32[8,4608]{1,0:T(8,128)S(1)}, f32[8,4608]{1,0:T(8,128)S(1)}, u32[]{:S(2)}, u32[]{:S(2)}) %collective-permute-start.7) | collective-permute-done | bytes 147488 | tf_op jit(solution)/shard_map/ppermute | solution.py:161
  21.3 2.2 %collective-permute-start.8 = (f32[8,4480]{1,0:T(8,128)S(1)}, f32[8,4480]{1,0:T(8,128)S(1)}, u32[]{:S(2)}, u32[]{:S(2)}) collective-permute-start(f32[8,4480]{1,0:T(8,128)S(1)} %shard_map.44.own_ref), channel_id=1, source_target_pairs={{0,4},{2,6},{4,0},{6,2},{8,12},{10,14},{12,8},{14,10},{1,5},{3,7},... | collective-permute-start | bytes 430088 | tf_op jit(solution)/shard_map/ppermute | solution.py:161
  23.4 0.4 collective-permute-done.10.partner_ref
  24.0 1.9 %collective-permute-start.11 = (f32[8,4480]{1,0:T(8,128)S(1)}, f32[8,4480]{1,0:T(8,128)S(1)}, u32[]{:S(2)}, u32[]{:S(2)}) collective-permute-start(f32[8,4480]{1,0:T(8,128)S(1)} %shard_map.47.own_ref), channel_id=1, source_target_pairs={{0,4},{2,6},{4,0},{6,2},{8,12},{10,14},{12,8},{14,10},{1,5},{3,7},... | collective-permute-start | bytes 430088 | tf_op jit(solution)/shard_map/ppermute | solution.py:161
  26.1 2.5 %collective-permute-start.3 = (f32[8,4352]{1,0:T(8,128)S(1)}, f32[8,4352]{1,0:T(8,128)S(1)}, u32[]{:S(2)}, u32[]{:S(2)}) collective-permute-start(f32[8,4352]{1,0:T(8,128)S(1)} %get-tuple-element.19), channel_id=1, source_target_pairs={{0,12},{2,14},{4,8},{6,10},{8,4},{10,6},{12,0},{14,2},{1,13},{3,15... | collective-permute-start | bytes 417800 | tf_op jit(solution)/shard_map/ppermute | solution.py:161
  28.9 1.4 %collective-permute-start.6 = (f32[8,4352]{1,0:T(8,128)S(1)}, f32[8,4352]{1,0:T(8,128)S(1)}, u32[]{:S(2)}, u32[]{:S(2)}) collective-permute-start(f32[8,4352]{1,0:T(8,128)S(1)} %get-tuple-element.22), channel_id=1, source_target_pairs={{0,12},{2,14},{4,8},{6,10},{8,4},{10,6},{12,0},{14,2},{1,13},{3,15... | collective-permute-start | bytes 417800 | tf_op jit(solution)/shard_map/ppermute | solution.py:161
  30.5 2.5 %collective-permute-start.9 = (f32[8,4352]{1,0:T(8,128)S(1)}, f32[8,4352]{1,0:T(8,128)S(1)}, u32[]{:S(2)}, u32[]{:S(2)}) collective-permute-start(f32[8,4352]{1,0:T(8,128)S(1)} %get-tuple-element.25), channel_id=1, source_target_pairs={{0,12},{2,14},{4,8},{6,10},{8,4},{10,6},{12,0},{14,2},{1,13},{3,15... | collective-permute-start | bytes 417800 | tf_op jit(solution)/shard_map/ppermute | solution.py:161
  33.3 11.1 %collective-permute-start.12 = (f32[8,4352]{1,0:T(8,128)S(1)}, f32[8,4352]{1,0:T(8,128)S(1)}, u32[]{:S(2)}, u32[]{:S(2)}) collective-permute-start(f32[8,4352]{1,0:T(8,128)S(1)} %get-tuple-element.28), channel_id=1, source_target_pairs={{0,12},{2,14},{4,8},{6,10},{8,4},{10,6},{12,0},{14,2},{1,13},{3,15... | collective-permute-start | bytes 417800 | tf_op jit(solution)/shard_map/ppermute | solution.py:161
  44.6 4.3 %shard_map.40 = f32[8,4096]{1,0:T(8,128)S(1)} custom-call(f32[8,4352]{1,0:T(8,128)S(1)} %get-tuple-element.18.own_ref, f32[8,4352]{1,0:T(8,128)S(1)} %collective-permute-done.3.partner_ref, s32[8,12]{1,0:T(8,128)S(1)} %get-tuple-element.29.table_ref, s32[24,128]{1,0:T(8,128)S(1)} %broadcast_in_dim.4.width_ref, f32[24,128]{1,0:T(8,128)S(1)} %broadcast_in_dim.5.weight_ref), custom_call_target="tpu_custom_call" | custom-call | tf_op jit(solution)/shard_map/pallas_call | solution.py:149
  48.8 4.3 %shard_map.43 = f32[8,4096]{1,0:T(8,128)S(1)} custom-call(f32[8,4352]{1,0:T(8,128)S(1)} %get-tuple-element.21.own_ref, f32[8,4352]{1,0:T(8,128)S(1)} %collective-permute-done.6.partner_ref, s32[8,12]{1,0:T(8,128)S(1)} %get-tuple-element.32.table_ref, s32[24,128]{1,0:T(8,128)S(1)} %broadcast_in_dim.4.width_ref, f32[24,128]{1,0:T(8,128)S(1)} %broadcast_in_dim.5.weight_ref), custom_call_target="tpu_custom_call" | custom-call | tf_op jit(solution)/shard_map/pallas_call | solution.py:149
  53.1 4.3 %shard_map.46 = f32[8,4096]{1,0:T(8,128)S(1)} custom-call(f32[8,4352]{1,0:T(8,128)S(1)} %get-tuple-element.24.own_ref, f32[8,4352]{1,0:T(8,128)S(1)} %collective-permute-done.9.partner_ref, s32[8,12]{1,0:T(8,128)S(1)} %get-tuple-element.31.table_ref, s32[24,128]{1,0:T(8,128)S(1)} %broadcast_in_dim.4.width_ref, f32[24,128]{1,0:T(8,128)S(1)} %broadcast_in_dim.5.weight_ref), custom_call_target="tpu_custom_call" | custom-call | tf_op jit(solution)/shard_map/pallas_call | solution.py:149
  57.4 4.3 %shard_map.49 = f32[8,4096]{1,0:T(8,128)S(1)} custom-call(f32[8,4352]{1,0:T(8,128)S(1)} %get-tuple-element.27.own_ref, f32[8,4352]{1,0:T(8,128)S(1)} %collective-permute-done.12.partner_ref, s32[8,12]{1,0:T(8,128)S(1)} %get-tuple-element.30.table_ref, s32[24,128]{1,0:T(8,128)S(1)} %broadcast_in_dim.4.width_ref, f32[24,128]{1,0:T(8,128)S(1)} %broadcast_in_dim.5.weight_ref), custom_call_target="tpu_custom_call" | custom-call | tf_op jit(solution)/shard_map/pallas_call | solution.py:149
  61.7 0.8 %pad_maximum_fusion = f32[32,4096]{1,0:T(8,128)} fusion(f32[8,4096]{1,0:T(8,128)S(1)} %shard_map.49, f32[8,4096]{1,0:T(8,128)S(1)} %shard_map.46, f32[8,4096]{1,0:T(8,128)S(1)} %shard_map.43, f32[8,4096]{1,0:T(8,128)S(1)} %shard_map.40), kind=kLoop, calls=%fused_computation | loop fusion | flops 393216 | bytes 1048576 | tf_op jit(solution)/shard_map/concatenate | solution.py:202
  (36 shorter events, 2.3 us)
Async XLA Ops:
  0.9 3.5 %collective-permute-start = (f32[32,1024]{1,0:T(8,128)S(1)}, f32[32,1024]{1,0:T(8,128)S(1)}, u32[]{:S(2)}, u32[]{:S(2)}) collective-permute-start(f32[32,1024]{1,0:T(8,128)S(1)} %slice.20), channel_id=1, source_target_pairs={{0,1},{2,3},{4,5},{6,7},{8,9},{10,11},{12,13},{14,15},{16,17},{18,... | collective-permute-start | bytes 393224 | tf_op jit(solution)/shard_map/ppermute | solution.py:174
  3.3 0.7 %copy-start.1 = (s32[8,256]{1,0:T(8,128)S(1)}, s32[8,256]{1,0:T(8,128)}, u32[]{:S(2)}) copy-start(s32[8,256]{1,0:T(8,128)} %param.4) | copy-start | bytes 24580
  4.4 1.0 %copy-start = (f32[32,4096]{1,0:T(8,128)S(1)}, f32[32,4096]{1,0:T(8,128)}, u32[]{:S(2)}) copy-start(f32[32,4096]{1,0:T(8,128)} %x_ref.1) | copy-start | bytes 1572868
  7.7 7.1 %collective-permute-start.1 = (f32[8,4608]{1,0:T(8,128)S(1)}, f32[8,4608]{1,0:T(8,128)S(1)}, u32[]{:S(2)}, u32[]{:S(2)}) collective-permute-start(f32[8,4608]{1,0:T(8,128)S(1)} %get-tuple-element.17.own_ref), channel_id=1, source_target_pairs={{0,2},{2,0},{4,6},{6,4},{8,10},{10,8},{12,14},{14,12},{1,3},{3,1},... | collective-permute-start | bytes 442376 | tf_op jit(solution)/shard_map/ppermute | solution.py:161
  10.1 7.9 %collective-permute-start.4 = (f32[8,4608]{1,0:T(8,128)S(1)}, f32[8,4608]{1,0:T(8,128)S(1)}, u32[]{:S(2)}, u32[]{:S(2)}) collective-permute-start(f32[8,4608]{1,0:T(8,128)S(1)} %get-tuple-element.20.own_ref), channel_id=1, source_target_pairs={{0,2},{2,0},{4,6},{6,4},{8,10},{10,8},{12,14},{14,12},{1,3},{3,1},... | collective-permute-start | bytes 442376 | tf_op jit(solution)/shard_map/ppermute | solution.py:161
  10.1 10.9 %collective-permute-start.7 = (f32[8,4608]{1,0:T(8,128)S(1)}, f32[8,4608]{1,0:T(8,128)S(1)}, u32[]{:S(2)}, u32[]{:S(2)}) collective-permute-start(f32[8,4608]{1,0:T(8,128)S(1)} %get-tuple-element.23.own_ref), channel_id=1, source_target_pairs={{0,2},{2,0},{4,6},{6,4},{8,10},{10,8},{12,14},{14,12},{1,3},{3,1},... | collective-permute-start | bytes 442376 | tf_op jit(solution)/shard_map/ppermute | solution.py:161
  12.1 11.7 %collective-permute-start.10 = (f32[8,4608]{1,0:T(8,128)S(1)}, f32[8,4608]{1,0:T(8,128)S(1)}, u32[]{:S(2)}, u32[]{:S(2)}) collective-permute-start(f32[8,4608]{1,0:T(8,128)S(1)} %get-tuple-element.26.own_ref), channel_id=1, source_target_pairs={{0,2},{2,0},{4,6},{6,4},{8,10},{10,8},{12,14},{14,12},{1,3},{3,1},... | collective-permute-start | bytes 442376 | tf_op jit(solution)/shard_map/ppermute | solution.py:161
  14.9 11.0 %collective-permute-start.2 = (f32[8,4480]{1,0:T(8,128)S(1)}, f32[8,4480]{1,0:T(8,128)S(1)}, u32[]{:S(2)}, u32[]{:S(2)}) collective-permute-start(f32[8,4480]{1,0:T(8,128)S(1)} %shard_map.38.own_ref), channel_id=1, source_target_pairs={{0,4},{2,6},{4,0},{6,2},{8,12},{10,14},{12,8},{14,10},{1,5},{3,7},... | collective-permute-start | bytes 430088 | tf_op jit(solution)/shard_map/ppermute | solution.py:161
  18.1 10.6 %collective-permute-start.5 = (f32[8,4480]{1,0:T(8,128)S(1)}, f32[8,4480]{1,0:T(8,128)S(1)}, u32[]{:S(2)}, u32[]{:S(2)}) collective-permute-start(f32[8,4480]{1,0:T(8,128)S(1)} %shard_map.41.own_ref), channel_id=1, source_target_pairs={{0,4},{2,6},{4,0},{6,2},{8,12},{10,14},{12,8},{14,10},{1,5},{3,7},... | collective-permute-start | bytes 430088 | tf_op jit(solution)/shard_map/ppermute | solution.py:161
  21.3 9.1 %collective-permute-start.8 = (f32[8,4480]{1,0:T(8,128)S(1)}, f32[8,4480]{1,0:T(8,128)S(1)}, u32[]{:S(2)}, u32[]{:S(2)}) collective-permute-start(f32[8,4480]{1,0:T(8,128)S(1)} %shard_map.44.own_ref), channel_id=1, source_target_pairs={{0,4},{2,6},{4,0},{6,2},{8,12},{10,14},{12,8},{14,10},{1,5},{3,7},... | collective-permute-start | bytes 430088 | tf_op jit(solution)/shard_map/ppermute | solution.py:161
  24.0 9.1 %collective-permute-start.11 = (f32[8,4480]{1,0:T(8,128)S(1)}, f32[8,4480]{1,0:T(8,128)S(1)}, u32[]{:S(2)}, u32[]{:S(2)}) collective-permute-start(f32[8,4480]{1,0:T(8,128)S(1)} %shard_map.47.own_ref), channel_id=1, source_target_pairs={{0,4},{2,6},{4,0},{6,2},{8,12},{10,14},{12,8},{14,10},{1,5},{3,7},... | collective-permute-start | bytes 430088 | tf_op jit(solution)/shard_map/ppermute | solution.py:161
  26.1 18.3 %collective-permute-start.3 = (f32[8,4352]{1,0:T(8,128)S(1)}, f32[8,4352]{1,0:T(8,128)S(1)}, u32[]{:S(2)}, u32[]{:S(2)}) collective-permute-start(f32[8,4352]{1,0:T(8,128)S(1)} %get-tuple-element.19), channel_id=1, source_target_pairs={{0,12},{2,14},{4,8},{6,10},{8,4},{10,6},{12,0},{14,2},{1,13},{3,15... | collective-permute-start | bytes 417800 | tf_op jit(solution)/shard_map/ppermute | solution.py:161
  28.9 19.9 %collective-permute-start.6 = (f32[8,4352]{1,0:T(8,128)S(1)}, f32[8,4352]{1,0:T(8,128)S(1)}, u32[]{:S(2)}, u32[]{:S(2)}) collective-permute-start(f32[8,4352]{1,0:T(8,128)S(1)} %get-tuple-element.22), channel_id=1, source_target_pairs={{0,12},{2,14},{4,8},{6,10},{8,4},{10,6},{12,0},{14,2},{1,13},{3,15... | collective-permute-start | bytes 417800 | tf_op jit(solution)/shard_map/ppermute | solution.py:161
  30.5 22.6 %collective-permute-start.9 = (f32[8,4352]{1,0:T(8,128)S(1)}, f32[8,4352]{1,0:T(8,128)S(1)}, u32[]{:S(2)}, u32[]{:S(2)}) collective-permute-start(f32[8,4352]{1,0:T(8,128)S(1)} %get-tuple-element.25), channel_id=1, source_target_pairs={{0,12},{2,14},{4,8},{6,10},{8,4},{10,6},{12,0},{14,2},{1,13},{3,15... | collective-permute-start | bytes 417800 | tf_op jit(solution)/shard_map/ppermute | solution.py:161
  33.3 11.1 %copy-start.2 = (s32[20]{0:T(128)S(1)}, s32[20]{0:T(128)}, u32[]{:S(2)}) copy-start(s32[20]{0:T(128)} %param.5) | copy-start | bytes 244
  33.3 24.0 %collective-permute-start.12 = (f32[8,4352]{1,0:T(8,128)S(1)}, f32[8,4352]{1,0:T(8,128)S(1)}, u32[]{:S(2)}, u32[]{:S(2)}) collective-permute-start(f32[8,4352]{1,0:T(8,128)S(1)} %get-tuple-element.28), channel_id=1, source_target_pairs={{0,12},{2,14},{4,8},{6,10},{8,4},{10,6},{12,0},{14,2},{1,13},{3,15... | collective-permute-start | bytes 417800 | tf_op jit(solution)/shard_map/ppermute | solution.py:161

commit v2 on v1

v2 whole, which is shorter than its diff:
```python
import functools

import jax
import jax.numpy as jnp
from jax import lax
from jax.experimental import pallas as pl
from jax.experimental.pallas import tpu as pltpu
from jax.sharding import PartitionSpec as P


LOCAL_SECTIONS = 5
SWAP_SECTIONS = 3
SECTIONS = LOCAL_SECTIONS + SWAP_SECTIONS
SHIFT_MAX = 112
WMAX = 128
NBOX = 20
LANES = 128
SUB = 8
NBOX_PAD = -(-NBOX // SUB) * SUB
FILTERS_AT_ONCE = 5
OUTPUTS_AT_ONCE = 12

MAIN_LOCAL = -(-LOCAL_SECTIONS * SHIFT_MAX // LANES)
TAIL = -(-(SECTIONS * SHIFT_MAX + WMAX) // LANES)
HEAD = [-(-((SWAP_SECTIONS - i) * SHIFT_MAX + WMAX) // LANES) for i in range(SWAP_SECTIONS + 1)]
MAIN = [MAIN_LOCAL + i for i in range(SWAP_SECTIONS + 2)]


def cols(k):
    return slice(k * LANES, (k + 1) * LANES)


def group_rows(g):
    return slice(g * SUB, (g + 1) * SUB)


def delay_tables(column):
    delay = jnp.broadcast_to(column, (SUB, LANES))
    lane = lax.broadcasted_iota(jnp.int32, (SUB, LANES), 1)
    return (lane - delay) & (LANES - 1), lane < LANES - delay


def shifted(newer, older, tables):
    take, fresh = tables
    mixed = jnp.where(fresh, newer, older)
    return jnp.take_along_axis(mixed, take, axis=1, mode="promise_in_bounds")


def local_sections(groups, table_ref, read_input, buffers, first_input, first_output, end, write):
    sub = lax.broadcasted_iota(jnp.int32, (SUB, LANES), 0)

    def read(level, g, k):
        if level == 0:
            return read_input(g, k)
        return buffers[(level - 1) % 2][group_rows(g), cols(k - first_input)]

    for level in range(LOCAL_SECTIONS):
        first = max(first_input, first_output - (LOCAL_SECTIONS - 1 - level))
        for g in range(groups):
            tables = delay_tables(table_ref[group_rows(g), level : level + 1])

            def pair(k):
                if 1 << level < SUB:
                    stride = 1 << level
                    own_bit = (sub >> level & 1) == 1
                    own = read(level, g, k)
                    lower = jnp.where(own_bit, pltpu.roll(own, stride, 0), own)
                    return lower, jnp.where(own_bit, own, pltpu.roll(own, SUB - stride, 0))
                stride = (1 << level) // SUB
                return read(level, g & ~stride, k), read(level, g | stride, k)

            older = pair(first - 1)[1] if first > first_input else jnp.zeros((SUB, LANES), jnp.float32)
            for k in range(first, end):
                lower, upper = pair(k)
                value = lower + shifted(upper, older, tables)
                older = upper
                if level < LOCAL_SECTIONS - 1:
                    buffers[level % 2][group_rows(g), cols(k - first_input)] = value
                else:
                    write(g, k, value)


def main_local_kernel(x_hbm, table_ref, *rest):
    groups = x_hbm.shape[0] // SUB
    outs, first_ref, (x_ref, *buffers, arrived) = rest[:groups], rest[groups], rest[groups + 1 :]
    copies = [pltpu.make_async_copy(x_hbm.at[group_rows(g), :], x_ref.at[group_rows(g), :], arrived.at[g]) for g in range(groups)]
    for copy in copies:
        copy.start()
    for copy in copies:
        copy.wait()

    def write(g, k, value):
        outs[g][:, cols(k - MAIN[0])] = value

    read = lambda g, k: x_ref[group_rows(g), cols(k)]
    local_sections(groups, table_ref, read, buffers, 0, MAIN[0], x_ref.shape[1] // LANES, write)
    first_ref[...] = x_ref[:, : MAIN[0] * LANES]


def head_local_kernel(earlier_ref, x_ref, table_ref, out_ref, *buffers):
    def read(g, k):
        ref, first = (earlier_ref, -TAIL) if k < 0 else (x_ref, 0)
        return ref[group_rows(g), cols(k - first)]

    def write(g, k, value):
        out_ref[group_rows(g), cols(k + HEAD[0])] = value

    local_sections(x_ref.shape[0] // SUB, table_ref, read, buffers, -TAIL, -HEAD[0], MAIN[0], write)


def bit_mask(table_ref, g, column):
    return jnp.broadcast_to(table_ref[group_rows(g), column : column + 1], (SUB, LANES)) == 1


def readers(section, heads, mains):
    def reader(side):
        def read(g, k):
            if k < MAIN[section]:
                return heads[side][group_rows(g), cols(k + HEAD[section])]
            return mains[side][g][:, cols(k - MAIN[section])]

        return read

    return reader(0), reader(1)


def swap_section(read_own, read_partner, table_ref, g, section, column, first, end, write):
    upper_own = bit_mask(table_ref, g, SECTIONS + section)
    tables = delay_tables(table_ref[group_rows(g), column : column + 1])
    older = None
    for k in range(first - 1, end):
        own, partner = read_own(g, k), read_partner(g, k)
        upper = jnp.where(upper_own, own, partner)
        if k >= first:
            write(g, k, jnp.where(upper_own, partner, own) + shifted(upper, older, tables))
        older = upper


def split_refs(section, groups, has_head, refs):
    heads = refs[:2] if has_head else None
    refs = refs[2 if has_head else 0 :]
    return readers(section, heads, (refs[:groups], refs[groups : 2 * groups])), refs[2 * groups :]


def swap_kernel(section, groups, first, end, *refs):
    has_head = first < MAIN[section]
    (read_own, read_partner), (table_ref, out_ref, *_) = split_refs(section, groups, has_head, refs)

    def write(g, k, value):
        out_ref[group_rows(g), cols(k - first)] = value

    for g in range(groups):
        swap_section(read_own, read_partner, table_ref, g, section, LOCAL_SECTIONS + section, first, end, write)


def power_kernel(section, groups, first, end, *refs):
    has_head = first - 2 < MAIN[section]
    (read_own, read_partner), (table_ref, width_ref, weight_ref, *rest) = split_refs(section, groups, has_head, refs)
    out_ref, prefix, suffix = rest[-3:]
    pieces = {}

    def keep(g, k, value):
        pieces[k, g] = value

    for g in range(groups):
        swap_section(read_own, read_partner, table_ref, g, section, LOCAL_SECTIONS + section, first - 1, end, keep)
    order = sorted(pieces)
    place = {key: i for i, key in enumerate(order)}
    series = jnp.concatenate([pieces[key] for key in order], axis=0)
    source = lax.broadcasted_iota(jnp.int32, (LANES, 2 * LANES), 0)
    target = lax.broadcasted_iota(jnp.int32, (LANES, 2 * LANES), 1)
    summing = jnp.where(target < LANES, jnp.where(source <= target, 1.0, 0.0), jnp.where(source > target - LANES, -1.0, 0.0))
    sums = jnp.dot(series, summing, precision=lax.Precision.HIGHEST, preferred_element_type=jnp.float32)
    prefix[...] = sums[:, :LANES]
    suffix[...] = sums[:, LANES:]
    lane = lax.broadcasted_iota(jnp.int32, (SUB, LANES), 1)
    outputs = [(k, g) for k in range(first, end) for g in range(groups)]

    for start in range(0, len(outputs), OUTPUTS_AT_ONCE):
        block = outputs[start : start + OUTPUTS_AT_ONCE]

        def add_filters(step, summed):
            for i in range(FILTERS_AT_ONCE):
                f = step * FILTERS_AT_ONCE + i
                width = jnp.broadcast_to(width_ref[pl.ds(f, 1), :], (SUB, LANES))
                weight = jnp.broadcast_to(weight_ref[pl.ds(f, 1), :], (SUB, LANES))
                tables = (lane - width) & (LANES - 1), lane < LANES - width
                updated = []
                for (k, g), value in zip(block, summed):
                    here = prefix[group_rows(place[k, g]), :]
                    window = here - shifted(here, suffix[group_rows(place[k - 1, g]), :], tables)
                    updated.append(value + window * window * weight)
                summed = tuple(updated)
            return summed

        zero = jnp.zeros((SUB, LANES), jnp.float32)
        summed = lax.fori_loop(0, NBOX // FILTERS_AT_ONCE, add_filters, (zero,) * len(block))
        for (k, g), value in zip(block, summed):
            out_ref[group_rows(g), cols(k - first)] = value


VMEM_BLOCK = pl.BlockSpec(memory_space=pltpu.VMEM)


class Ordered:
    def __init__(self):
        self.previous = ()

    def __call__(self, kernel, args, out_shapes, scratch=(), spaces=None):
        count, unread = len(args), len(self.previous)

        def body(*refs):
            kernel(*refs[:count], *refs[count + unread :])

        outs = list(pl.pallas_call(
            body,
            out_shape=[jax.ShapeDtypeStruct(shape, jnp.float32) for shape in out_shapes],
            in_specs=(spaces or [VMEM_BLOCK] * count) + [pl.BlockSpec(memory_space=pl.ANY)] * unread,
            out_specs=[VMEM_BLOCK] * len(out_shapes),
            scratch_shapes=[pltpu.VMEM(s, jnp.float32) if isinstance(s, tuple) else s for s in scratch],
            compiler_params=pltpu.CompilerParams(vmem_limit_bytes=8 << 20),
        )(*args, *self.previous))
        self.previous = (outs[0],)
        return outs


def swapped(block, flip):
    count = lax.axis_size("chan")
    return lax.ppermute(block, "chan", [(i, i ^ flip) for i in range(count)])


def local(spectra, delay_shifts, box_widths):
    ch_rows, time_len = spectra.shape
    groups = ch_rows // SUB
    end = time_len // LANES
    steps = lax.axis_size("tm")
    me = lax.axis_index("chan")
    chan_bits = lax.axis_size("chan").bit_length() - 1
    bits = [1 << (chan_bits - SWAP_SECTIONS + i) for i in range(SWAP_SECTIONS)]

    earlier = lax.ppermute(spectra[:, -TAIL * LANES :], "tm", [(i, i + 1) for i in range(steps - 1)])

    own_shifts = lax.dynamic_slice_in_dim(delay_shifts, me * ch_rows, ch_rows, 1)
    own_bits = jnp.stack([jnp.broadcast_to((me & bit != 0).astype(jnp.int32), (ch_rows,)) for bit in bits])
    table = jnp.concatenate([own_shifts, own_bits]).T
    widths = jnp.concatenate([box_widths, jnp.full((NBOX_PAD - NBOX,), WMAX, jnp.int32)])
    weights = 1.0 / (widths.astype(jnp.float32) * (NBOX * 2.0**SECTIONS))
    widths = jnp.broadcast_to(widths[:, None], (NBOX_PAD, LANES))
    weights = jnp.broadcast_to(weights[:, None], (NBOX_PAD, LANES))

    call = Ordered()
    shape = lambda rows, chunks: (rows, chunks * LANES)
    wide = shape(ch_rows, end)
    narrow = shape(ch_rows, TAIL + MAIN[0])
    tables = [table[group_rows(g)] for g in range(groups)]
    filters = (widths, weights)
    cut = MAIN[SWAP_SECTIONS] + 1
    last = SWAP_SECTIONS - 1

    shapes = [shape(SUB, end - MAIN[0])] * groups + [shape(ch_rows, MAIN[0])]
    scratch = (wide, wide, wide, pltpu.SemaphoreType.DMA((groups,)))
    *pieces, first = call(main_local_kernel, (spectra, table), shapes, scratch, [pl.BlockSpec(memory_space=pltpu.HBM), VMEM_BLOCK])
    head = call(head_local_kernel, (earlier, first, table), [shape(ch_rows, HEAD[0] + MAIN[0])], (narrow, narrow))
    mains = [pieces]
    main_peers = [[swapped(piece, bits[0]) for piece in mains[0]]]
    head_peer = [swapped(head[0], bits[0])]

    def main_step(section, g):
        args = (mains[section][g], main_peers[section][g], tables[g])
        if section < last:
            first = MAIN[section + 1]
            (piece,) = call(functools.partial(swap_kernel, section, 1, first, end), args, [shape(SUB, end - first)])
            if g == 0:
                mains.append([])
                main_peers.append([])
            mains[section + 1].append(piece)
            main_peers[section + 1].append(swapped(piece, bits[section + 1]))
        else:
            kernel = functools.partial(power_kernel, section, 1, cut, end)
            results.extend(call(kernel, args + filters, [shape(SUB, end - cut)], [(SUB * (end - cut + 1), LANES)] * 2))

    def head_step(section):
        args = (head[section], head_peer[section], *mains[section], *main_peers[section], table)
        if section < last:
            first, stop = -HEAD[section + 1], MAIN[section + 1]
            head.extend(call(functools.partial(swap_kernel, section, groups, first, stop), args, [shape(ch_rows, stop - first)]))
            head_peer.append(swapped(head[section + 1], bits[section + 1]))
        else:
            kernel = functools.partial(power_kernel, section, groups, 0, cut)
            head.extend(call(kernel, args + filters, [shape(ch_rows, cut)], [(SUB * groups * (cut + 1), LANES)] * 2))

    results = []
    for section, g in work_order(PIECES):
        main_step(section, g) if g < groups else head_step(section)
    return jnp.concatenate([head[-1], jnp.concatenate(results, axis=0)], axis=1)


def work_order(pieces):
    keys = [(g + LAG[section], section, g) for section in range(SWAP_SECTIONS) for g in range(pieces)]
    return [(section, g) for _, section, g in sorted(keys)]


LAG = [0, 1.5, 4.2]
PIECES = 5


def solution(mesh):
    in_specs = (P(("beam", "chan"), "tm"), P(), P())
    out_specs = P(("beam", "chan"), "tm")
    return jax.shard_map(local, mesh=mesh, in_specs=in_specs, out_specs=out_specs, check_vma=False)
```

time: 62.7 us -> 58.4 us (0.931)
  waiting for transfers between devices: 4.6 us -> 18.8 us
  starting transfers between devices: 32.8 us -> 21.9 us
  Pallas kernels: 20.9 us -> 13.9 us
    ppermute x12 -> x15, waiting for transfers between devices: 4.6 us -> 18.8 us  [swapped(): return lax.ppermute(block, 'chan', [(i, i ^ flip) for i in range(count)])]
    ppermute x12 -> x15, starting transfers between devices: 30.4 us -> 19.5 us  [swapped(): return lax.ppermute(block, 'chan', [(i, i ^ flip) for i in range(count)])]
    pallas_call x13 -> x17, Pallas kernels: 20.9 us -> 13.9 us  [__call__(): pl.pallas_call(body, out_shape=[jax.ShapeDtypeStruct(shape, jnp.float32)...]
    unnamed x8 -> x7, local copies, waits for them, and re-layouts: 1.9 us -> 1.13 us
  transfers between devices with their start and end apart: 13 -> 16, of which waited for: 4 -> 7; matrix products, arithmetic and copies ran while one was open for 1% -> 1% of each run, Pallas kernels for 23% -> 19%
where the time goes in v2:
time: 58.4 us; the launch traced here: 58.2 us
  starting transfers between devices  21.9 us (38%)
  waiting for transfers between devices  18.8 us (32%)
  Pallas kernels  13.9 us (24%)
  local copies, waits for them, and re-layouts  2.5 us (4%)
  other arithmetic  0.86 us (1%)
    ppermute x15, starting transfers between devices, swapped(): return lax.ppermute(block, 'chan', [(i, i ^ flip) for i in range(count)])  19.5 us
    ppermute x15, waiting for transfers between devices, swapped(): return lax.ppermute(block, 'chan', [(i, i ^ flip) for i in range(count)])  18.8 us
    pallas_call x17, Pallas kernels, __call__(): pl.pallas_call(body, out_shape=[jax.ShapeDtypeStruct(shape, jnp.float32)...  13.9 us
    ppermute x1, starting transfers between devices, local(): lax.ppermute(spectra[:, -TAIL * LANES:], 'tm', [(i, i + 1) for i in range...  2.4 us
  transfers between devices with their start and end apart: 16, of which 7 were waited for; matrix products, arithmetic and copies ran while one was open for 1% of the time, Pallas kernels for 19%

profile of v2, /device:TPU:0, one launch (start us, length us, event | category | flops | bytes accessed | tf_op | source)
XLA Modules:
  0.0 58.2 jit_solution(7770006839174681161)
XLA Ops:
  0.9 2.4 %collective-permute-start = (f32[32,1024]{1,0:T(8,128)S(1)}, f32[32,1024]{1,0:T(8,128)S(1)}, u32[]{:S(2)}, u32[]{:S(2)}) collective-permute-start(f32[32,1024]{1,0:T(8,128)S(1)} %slice.15), channel_id=1, source_target_pairs={{0,1},{2,3},{4,5},{6,7},{8,9},{10,11},{12,13},{14,15},{16,17},{18,... | collective-permute-start | bytes 393224 | tf_op jit(solution)/shard_map/ppermute | solution.py:241
  3.8 1.0 %copy-done.1 = f32[32,4096]{1,0:T(8,128)S(1)} copy-done((f32[32,4096]{1,0:T(8,128)S(1)}, f32[32,4096]{1,0:T(8,128)}, u32[]{:S(2)}) %copy-start.1) | copy-done | bytes 524312
  4.8 2.7 %shard_map.37 = (f32[8,3456]{1,0:T(8,128)S(1)}, f32[8,3456]{1,0:T(8,128)S(1)}, f32[8,3456]{1,0:T(8,128)S(1)}, f32[8,3456]{1,0:T(8,128)S(1)}, f32[32,640]{1,0:T(8,128)S(1)}) custom-call(f32[32,4096]{1,0:T(8,128)S(1)} %copy-done.1, s32[32,11]{1,0:T(8,128)S(1)} %add_bitcast_fusion.refs_1_.refs_2_.refs_10_), custom_call_target="tpu_custom_call" | custom-call | tf_op jit(solution)/shard_map/pallas_call | solution.py:215
  7.5 2.4 %collective-permute-start.2 = (f32[8,3456]{1,0:T(8,128)S(1)}, f32[8,3456]{1,0:T(8,128)S(1)}, u32[]{:S(2)}, u32[]{:S(2)}) collective-permute-start(f32[8,3456]{1,0:T(8,128)S(1)} %get-tuple-element.11.refs_3_.refs_0_.refs_2_), channel_id=1, source_target_pairs={{0,2},{2,0},{4,6},{6,4},{8,10},{10,8},{12,14},{14,12},{1,3},{3,1},... | collective-permute-start | bytes 331784 | tf_op jit(solution)/shard_map/ppermute | solution.py:229
  9.9 1.9 %collective-permute-start.4 = (f32[8,3456]{1,0:T(8,128)S(1)}, f32[8,3456]{1,0:T(8,128)S(1)}, u32[]{:S(2)}, u32[]{:S(2)}) collective-permute-start(f32[8,3456]{1,0:T(8,128)S(1)} %get-tuple-element.13.refs_0_.refs_4_), channel_id=1, source_target_pairs={{0,2},{2,0},{4,6},{6,4},{8,10},{10,8},{12,14},{14,12},{1,3},{3,1},... | collective-permute-start | bytes 331784 | tf_op jit(solution)/shard_map/ppermute | solution.py:229
  12.4 1.2 %collective-permute-done.2.refs_1_.refs_6_ = f32[8,3456]{1,0:T(8,128)S(1)} collective-permute-done((f32[8,3456]{1,0:T(8,128)S(1)}, f32[8,3456]{1,0:T(8,128)S(1)}, u32[]{:S(2)}, u32[]{:S(2)}) %collective-permute-start.2) | collective-permute-done | bytes 110624 | tf_op jit(solution)/shard_map/ppermute | solution.py:229
  13.8 2.3 %collective-permute-start.6 = (f32[8,3328]{1,0:T(8,128)S(1)}, f32[8,3328]{1,0:T(8,128)S(1)}, u32[]{:S(2)}, u32[]{:S(2)}) collective-permute-start(f32[8,3328]{1,0:T(8,128)S(1)} %shard_map.39.refs_3_.refs_0_.refs_2_), channel_id=1, source_target_pairs={{0,4},{2,6},{4,0},{6,2},{8,12},{10,14},{12,8},{14,10},{1,5},{3,7},... | collective-permute-start | bytes 319496 | tf_op jit(solution)/shard_map/ppermute | solution.py:229
  16.1 1.5 %collective-permute-start.1 = (f32[32,1152]{1,0:T(8,128)S(1)}, f32[32,1152]{1,0:T(8,128)S(1)}, u32[]{:S(2)}, u32[]{:S(2)}) collective-permute-start(f32[32,1152]{1,0:T(8,128)S(1)} %shard_map.38.refs_3_.refs_0_), channel_id=1, source_target_pairs={{0,2},{2,0},{4,6},{6,4},{8,10},{10,8},{12,14},{14,12},{1,3},{3,1},... | collective-permute-start | bytes 442376 | tf_op jit(solution)/shard_map/ppermute | solution.py:229
  18.5 1.2 %collective-permute-done.6.refs_1_.refs_6_ = f32[8,3328]{1,0:T(8,128)S(1)} collective-permute-done((f32[8,3328]{1,0:T(8,128)S(1)}, f32[8,3328]{1,0:T(8,128)S(1)}, u32[]{:S(2)}, u32[]{:S(2)}) %collective-permute-start.6) | collective-permute-done | bytes 106528 | tf_op jit(solution)/shard_map/ppermute | solution.py:229
  20.0 1.6 %collective-permute-start.7 = (f32[8,3328]{1,0:T(8,128)S(1)}, f32[8,3328]{1,0:T(8,128)S(1)}, u32[]{:S(2)}, u32[]{:S(2)}) collective-permute-start(f32[8,3328]{1,0:T(8,128)S(1)} %shard_map.42.refs_3_.refs_0_.refs_4_), channel_id=1, source_target_pairs={{0,4},{2,6},{4,0},{6,2},{8,12},{10,14},{12,8},{14,10},{1,5},{3,7},... | collective-permute-start | bytes 319496 | tf_op jit(solution)/shard_map/ppermute | solution.py:229
  21.6 1.5 %collective-permute-done.8.refs_1_.refs_7_ = f32[8,3328]{1,0:T(8,128)S(1)} collective-permute-done((f32[8,3328]{1,0:T(8,128)S(1)}, f32[8,3328]{1,0:T(8,128)S(1)}, u32[]{:S(2)}, u32[]{:S(2)}) %collective-permute-start.8) | collective-permute-done | bytes 106528 | tf_op jit(solution)/shard_map/ppermute | solution.py:229
  23.4 1.6 %collective-permute-done.7.refs_1_.refs_8_ = f32[8,3328]{1,0:T(8,128)S(1)} collective-permute-done((f32[8,3328]{1,0:T(8,128)S(1)}, f32[8,3328]{1,0:T(8,128)S(1)}, u32[]{:S(2)}, u32[]{:S(2)}) %collective-permute-start.7) | collective-permute-done | bytes 106528 | tf_op jit(solution)/shard_map/ppermute | solution.py:229
  25.4 1.4 %collective-permute-start.9 = (f32[32,1152]{1,0:T(8,128)S(1)}, f32[32,1152]{1,0:T(8,128)S(1)}, u32[]{:S(2)}, u32[]{:S(2)}) collective-permute-start(f32[32,1152]{1,0:T(8,128)S(1)} %shard_map.46.refs_5_.refs_0_), channel_id=1, source_target_pairs={{0,4},{2,6},{4,0},{6,2},{8,12},{10,14},{12,8},{14,10},{1,5},{3,7},... | collective-permute-start | bytes 442376 | tf_op jit(solution)/shard_map/ppermute | solution.py:229
  26.8 2.6 %collective-permute-start.12 = (f32[8,3200]{1,0:T(8,128)S(1)}, f32[8,3200]{1,0:T(8,128)S(1)}, u32[]{:S(2)}, u32[]{:S(2)}) collective-permute-start(f32[8,3200]{1,0:T(8,128)S(1)} %shard_map.41.refs_3_.refs_0_.refs_2_), channel_id=1, source_target_pairs={{0,8},{2,10},{4,12},{6,14},{8,0},{10,2},{12,4},{14,6},{1,9},{3,11}... | collective-permute-start | bytes 307208 | tf_op jit(solution)/shard_map/ppermute | solution.py:229
  29.4 1.5 %collective-permute-start.10 = (f32[8,3328]{1,0:T(8,128)S(1)}, f32[8,3328]{1,0:T(8,128)S(1)}, u32[]{:S(2)}, u32[]{:S(2)}) collective-permute-start(f32[8,3328]{1,0:T(8,128)S(1)} %shard_map.44.refs_3_.refs_0_.refs_5_), channel_id=1, source_target_pairs={{0,4},{2,6},{4,0},{6,2},{8,12},{10,14},{12,8},{14,10},{1,5},{3,7},... | collective-permute-start | bytes 319496 | tf_op jit(solution)/shard_map/ppermute | solution.py:229
  30.9 2.3 %collective-permute-done.12.refs_1_.refs_6_ = f32[8,3200]{1,0:T(8,128)S(1)} collective-permute-done((f32[8,3200]{1,0:T(8,128)S(1)}, f32[8,3200]{1,0:T(8,128)S(1)}, u32[]{:S(2)}, u32[]{:S(2)}) %collective-permute-start.12) | collective-permute-done | bytes 102432 | tf_op jit(solution)/shard_map/ppermute | solution.py:229
  33.4 1.6 %shard_map.47.refs_3_ = f32[8,2944]{1,0:T(8,128)S(1)} custom-call(f32[8,3200]{1,0:T(8,128)S(1)} %shard_map.41.refs_3_.refs_0_.refs_2_, f32[8,3200]{1,0:T(8,128)S(1)} %collective-permute-done.12.refs_1_.refs_6_, s32[8,11]{1,0:T(8,128)S(1)} %get-tuple-element.18.refs_2_, s32[24,128]{1,0:T(8,128)S(1)} %broadcast_in_dim.4.refs_3_.refs_11_, ...), custom_call_target="tpu_custom_call" | custom-call | tf_op jit(solution)/shard_map/pallas_call | solution.py:215
  35.2 2.3 %collective-permute-done.11.refs_1_.refs_7_ = f32[8,3200]{1,0:T(8,128)S(1)} collective-permute-done((f32[8,3200]{1,0:T(8,128)S(1)}, f32[8,3200]{1,0:T(8,128)S(1)}, u32[]{:S(2)}, u32[]{:S(2)}) %collective-permute-start.11) | collective-permute-done | bytes 102432 | tf_op jit(solution)/shard_map/ppermute | solution.py:229
  37.5 1.6 %shard_map.49.refs_11_ = f32[8,2944]{1,0:T(8,128)S(1)} custom-call(f32[8,3200]{1,0:T(8,128)S(1)} %shard_map.43.refs_3_.refs_0_, f32[8,3200]{1,0:T(8,128)S(1)} %collective-permute-done.11.refs_1_.refs_7_, s32[8,11]{1,0:T(8,128)S(1)} %get-tuple-element.17.refs_2_, s32[24,128]{1,0:T(8,128)S(1)} %broadcast_in_dim.4.refs_3_.refs_11_, ...), custom_call_target="tpu_custom_call" | custom-call | tf_op jit(solution)/shard_map/pallas_call | solution.py:215
  39.9 2.4 %collective-permute-start.14 = (f32[8,3200]{1,0:T(8,128)S(1)}, f32[8,3200]{1,0:T(8,128)S(1)}, u32[]{:S(2)}, u32[]{:S(2)}) collective-permute-start(f32[8,3200]{1,0:T(8,128)S(1)} %shard_map.45.refs_11_.refs_0_.refs_4_), channel_id=1, source_target_pairs={{0,8},{2,10},{4,12},{6,14},{8,0},{10,2},{12,4},{14,6},{1,9},{3,11}... | collective-permute-start | bytes 307208 | tf_op jit(solution)/shard_map/ppermute | solution.py:229
  42.9 8.7 %collective-permute-done.14.refs_1_.refs_8_ = f32[8,3200]{1,0:T(8,128)S(1)} collective-permute-done((f32[8,3200]{1,0:T(8,128)S(1)}, f32[8,3200]{1,0:T(8,128)S(1)}, u32[]{:S(2)}, u32[]{:S(2)}) %collective-permute-start.14) | collective-permute-done | bytes 102432 | tf_op jit(solution)/shard_map/ppermute | solution.py:229
  51.6 1.6 %shard_map.51.refs_5_ = f32[8,2944]{1,0:T(8,128)S(1)} custom-call(f32[8,3200]{1,0:T(8,128)S(1)} %shard_map.45.refs_11_.refs_0_.refs_4_, f32[8,3200]{1,0:T(8,128)S(1)} %collective-permute-done.14.refs_1_.refs_8_, s32[8,11]{1,0:T(8,128)S(1)} %get-tuple-element.15.refs_2_, s32[24,128]{1,0:T(8,128)S(1)} %broadcast_in_dim.4.refs_3_.refs_11_, ...), custom_call_target="tpu_custom_call" | custom-call | tf_op jit(solution)/shard_map/pallas_call | solution.py:215
  53.2 1.6 %shard_map.52.refs_13_ = f32[8,2944]{1,0:T(8,128)S(1)} custom-call(f32[8,3200]{1,0:T(8,128)S(1)} %shard_map.48.refs_5_.refs_0_, f32[8,3200]{1,0:T(8,128)S(1)} %collective-permute-done.15.refs_1_.refs_9_, s32[8,11]{1,0:T(8,128)S(1)} %get-tuple-element.16.refs_2_, s32[24,128]{1,0:T(8,128)S(1)} %broadcast_in_dim.4.refs_3_.refs_11_, ...), custom_call_target="tpu_custom_call" | custom-call | tf_op jit(solution)/shard_map/pallas_call | solution.py:215
  54.9 2.4 %shard_map.53 = f32[32,1152]{1,0:T(8,128)S(1)} custom-call(f32[32,1152]{1,0:T(8,128)S(1)} %shard_map.50.refs_5_.refs_0_, f32[32,1152]{1,0:T(8,128)S(1)} %collective-permute-done.13.refs_1_, f32[8,3200]{1,0:T(8,128)S(1)} %shard_map.41.refs_3_.refs_0_.refs_2_, f32[8,3200]{1,0:T(8,128)S(1)} %shard_map.43.refs_3_.refs_0_, ...), custom_call_target="tpu_custom_call" | custom-call | tf_op jit(solution)/shard_map/pallas_call | solution.py:215
  (44 shorter events, 6.6 us)
Async XLA Ops:
  0.0 3.4 %copy-start = (s32[8,256]{1,0:T(8,128)S(1)}, s32[8,256]{1,0:T(8,128)}, u32[]{:S(2)}) copy-start(s32[8,256]{1,0:T(8,128)} %param.4) | copy-start | bytes 24580
  0.9 10.9 %collective-permute-start = (f32[32,1024]{1,0:T(8,128)S(1)}, f32[32,1024]{1,0:T(8,128)S(1)}, u32[]{:S(2)}, u32[]{:S(2)}) collective-permute-start(f32[32,1024]{1,0:T(8,128)S(1)} %slice.15), channel_id=1, source_target_pairs={{0,1},{2,3},{4,5},{6,7},{8,9},{10,11},{12,13},{14,15},{16,17},{18,... | collective-permute-start | bytes 393224 | tf_op jit(solution)/shard_map/ppermute | solution.py:241
  3.7 1.0 %copy-start.1 = (f32[32,4096]{1,0:T(8,128)S(1)}, f32[32,4096]{1,0:T(8,128)}, u32[]{:S(2)}) copy-start(f32[32,4096]{1,0:T(8,128)} %refs_0_.1) | copy-start | bytes 1572868
  7.5 6.1 %collective-permute-start.2 = (f32[8,3456]{1,0:T(8,128)S(1)}, f32[8,3456]{1,0:T(8,128)S(1)}, u32[]{:S(2)}, u32[]{:S(2)}) collective-permute-start(f32[8,3456]{1,0:T(8,128)S(1)} %get-tuple-element.11.refs_3_.refs_0_.refs_2_), channel_id=1, source_target_pairs={{0,2},{2,0},{4,6},{6,4},{8,10},{10,8},{12,14},{14,12},{1,3},{3,1},... | collective-permute-start | bytes 331784 | tf_op jit(solution)/shard_map/ppermute | solution.py:229
  9.8 8.3 %collective-permute-start.3 = (f32[8,3456]{1,0:T(8,128)S(1)}, f32[8,3456]{1,0:T(8,128)S(1)}, u32[]{:S(2)}, u32[]{:S(2)}) collective-permute-start(f32[8,3456]{1,0:T(8,128)S(1)} %get-tuple-element.12.refs_0_.refs_3_), channel_id=1, source_target_pairs={{0,2},{2,0},{4,6},{6,4},{8,10},{10,8},{12,14},{14,12},{1,3},{3,1},... | collective-permute-start | bytes 331784 | tf_op jit(solution)/shard_map/ppermute | solution.py:229
  9.9 9.9 %collective-permute-start.4 = (f32[8,3456]{1,0:T(8,128)S(1)}, f32[8,3456]{1,0:T(8,128)S(1)}, u32[]{:S(2)}, u32[]{:S(2)}) collective-permute-start(f32[8,3456]{1,0:T(8,128)S(1)} %get-tuple-element.13.refs_0_.refs_4_), channel_id=1, source_target_pairs={{0,2},{2,0},{4,6},{6,4},{8,10},{10,8},{12,14},{14,12},{1,3},{3,1},... | collective-permute-start | bytes 331784 | tf_op jit(solution)/shard_map/ppermute | solution.py:229
  13.8 5.9 %collective-permute-start.6 = (f32[8,3328]{1,0:T(8,128)S(1)}, f32[8,3328]{1,0:T(8,128)S(1)}, u32[]{:S(2)}, u32[]{:S(2)}) collective-permute-start(f32[8,3328]{1,0:T(8,128)S(1)} %shard_map.39.refs_3_.refs_0_.refs_2_), channel_id=1, source_target_pairs={{0,4},{2,6},{4,0},{6,2},{8,12},{10,14},{12,8},{14,10},{1,5},{3,7},... | collective-permute-start | bytes 319496 | tf_op jit(solution)/shard_map/ppermute | solution.py:229
  16.1 9.1 %collective-permute-start.1 = (f32[32,1152]{1,0:T(8,128)S(1)}, f32[32,1152]{1,0:T(8,128)S(1)}, u32[]{:S(2)}, u32[]{:S(2)}) collective-permute-start(f32[32,1152]{1,0:T(8,128)S(1)} %shard_map.38.refs_3_.refs_0_), channel_id=1, source_target_pairs={{0,2},{2,0},{4,6},{6,4},{8,10},{10,8},{12,14},{14,12},{1,3},{3,1},... | collective-permute-start | bytes 442376 | tf_op jit(solution)/shard_map/ppermute | solution.py:229
  17.6 5.7 %collective-permute-start.5 = (f32[8,3456]{1,0:T(8,128)S(1)}, f32[8,3456]{1,0:T(8,128)S(1)}, u32[]{:S(2)}, u32[]{:S(2)}) collective-permute-start(f32[8,3456]{1,0:T(8,128)S(1)} %get-tuple-element.14.refs_0_.refs_5_), channel_id=1, source_target_pairs={{0,2},{2,0},{4,6},{6,4},{8,10},{10,8},{12,14},{14,12},{1,3},{3,1},... | collective-permute-start | bytes 331784 | tf_op jit(solution)/shard_map/ppermute | solution.py:229
  18.3 4.8 %collective-permute-start.8 = (f32[8,3328]{1,0:T(8,128)S(1)}, f32[8,3328]{1,0:T(8,128)S(1)}, u32[]{:S(2)}, u32[]{:S(2)}) collective-permute-start(f32[8,3328]{1,0:T(8,128)S(1)} %shard_map.40.refs_3_.refs_0_), channel_id=1, source_target_pairs={{0,4},{2,6},{4,0},{6,2},{8,12},{10,14},{12,8},{14,10},{1,5},{3,7},... | collective-permute-start | bytes 319496 | tf_op jit(solution)/shard_map/ppermute | solution.py:229
  20.0 5.0 %collective-permute-start.7 = (f32[8,3328]{1,0:T(8,128)S(1)}, f32[8,3328]{1,0:T(8,128)S(1)}, u32[]{:S(2)}, u32[]{:S(2)}) collective-permute-start(f32[8,3328]{1,0:T(8,128)S(1)} %shard_map.42.refs_3_.refs_0_.refs_4_), channel_id=1, source_target_pairs={{0,4},{2,6},{4,0},{6,2},{8,12},{10,14},{12,8},{14,10},{1,5},{3,7},... | collective-permute-start | bytes 319496 | tf_op jit(solution)/shard_map/ppermute | solution.py:229
  25.2 1.6 %copy-start.2 = (s32[20]{0:T(128)S(1)}, s32[20]{0:T(128)}, u32[]{:S(2)}) copy-start(s32[20]{0:T(128)} %param.5) | copy-start | bytes 244
  25.4 13.7 %collective-permute-start.9 = (f32[32,1152]{1,0:T(8,128)S(1)}, f32[32,1152]{1,0:T(8,128)S(1)}, u32[]{:S(2)}, u32[]{:S(2)}) collective-permute-start(f32[32,1152]{1,0:T(8,128)S(1)} %shard_map.46.refs_5_.refs_0_), channel_id=1, source_target_pairs={{0,4},{2,6},{4,0},{6,2},{8,12},{10,14},{12,8},{14,10},{1,5},{3,7},... | collective-permute-start | bytes 442376 | tf_op jit(solution)/shard_map/ppermute | solution.py:229
  26.8 6.5 %collective-permute-start.12 = (f32[8,3200]{1,0:T(8,128)S(1)}, f32[8,3200]{1,0:T(8,128)S(1)}, u32[]{:S(2)}, u32[]{:S(2)}) collective-permute-start(f32[8,3200]{1,0:T(8,128)S(1)} %shard_map.41.refs_3_.refs_0_.refs_2_), channel_id=1, source_target_pairs={{0,8},{2,10},{4,12},{6,14},{8,0},{10,2},{12,4},{14,6},{1,9},{3,11}... | collective-permute-start | bytes 307208 | tf_op jit(solution)/shard_map/ppermute | solution.py:229
  29.4 5.7 %collective-permute-start.10 = (f32[8,3328]{1,0:T(8,128)S(1)}, f32[8,3328]{1,0:T(8,128)S(1)}, u32[]{:S(2)}, u32[]{:S(2)}) collective-permute-start(f32[8,3328]{1,0:T(8,128)S(1)} %shard_map.44.refs_3_.refs_0_.refs_5_), channel_id=1, source_target_pairs={{0,4},{2,6},{4,0},{6,2},{8,12},{10,14},{12,8},{14,10},{1,5},{3,7},... | collective-permute-start | bytes 319496 | tf_op jit(solution)/shard_map/ppermute | solution.py:229
  30.8 6.7 %collective-permute-start.11 = (f32[8,3200]{1,0:T(8,128)S(1)}, f32[8,3200]{1,0:T(8,128)S(1)}, u32[]{:S(2)}, u32[]{:S(2)}) collective-permute-start(f32[8,3200]{1,0:T(8,128)S(1)} %shard_map.43.refs_3_.refs_0_), channel_id=1, source_target_pairs={{0,8},{2,10},{4,12},{6,14},{8,0},{10,2},{12,4},{14,6},{1,9},{3,11}... | collective-permute-start | bytes 307208 | tf_op jit(solution)/shard_map/ppermute | solution.py:229
  39.4 15.5 %collective-permute-start.13 = (f32[32,1152]{1,0:T(8,128)S(1)}, f32[32,1152]{1,0:T(8,128)S(1)}, u32[]{:S(2)}, u32[]{:S(2)}) collective-permute-start(f32[32,1152]{1,0:T(8,128)S(1)} %shard_map.50.refs_5_.refs_0_), channel_id=1, source_target_pairs={{0,8},{2,10},{4,12},{6,14},{8,0},{10,2},{12,4},{14,6},{1,9},{3,11}... | collective-permute-start | bytes 442376 | tf_op jit(solution)/shard_map/ppermute | solution.py:229
  39.9 11.6 %collective-permute-start.14 = (f32[8,3200]{1,0:T(8,128)S(1)}, f32[8,3200]{1,0:T(8,128)S(1)}, u32[]{:S(2)}, u32[]{:S(2)}) collective-permute-start(f32[8,3200]{1,0:T(8,128)S(1)} %shard_map.45.refs_11_.refs_0_.refs_4_), channel_id=1, source_target_pairs={{0,8},{2,10},{4,12},{6,14},{8,0},{10,2},{12,4},{14,6},{1,9},{3,11}... | collective-permute-start | bytes 307208 | tf_op jit(solution)/shard_map/ppermute | solution.py:229
  42.3 10.9 %collective-permute-start.15 = (f32[8,3200]{1,0:T(8,128)S(1)}, f32[8,3200]{1,0:T(8,128)S(1)}, u32[]{:S(2)}, u32[]{:S(2)}) collective-permute-start(f32[8,3200]{1,0:T(8,128)S(1)} %shard_map.48.refs_5_.refs_0_), channel_id=1, source_target_pairs={{0,8},{2,10},{4,12},{6,14},{8,0},{10,2},{12,4},{14,6},{1,9},{3,11}... | collective-permute-start | bytes 307208 | tf_op jit(solution)/shard_map/ppermute | solution.py:229
